TPU v7x, 32 devices: a whole 2x2x4 slice. The times are simulated.
32 devices in a mesh: dp: 4 (over y, core), tensor: 8 (over z, x).
Axes of the slice: x: 2, y: 2, z: 4, core: 2. Of those that a mesh axis runs over, the one named last changes fastest.
Arguments:
- tokens: bfloat16 [8192, 2048], P(('dp', 'tensor')), may hold values from -6 to 6
- segment_ids: int32 [4, 2048], P('dp'), may hold values from 0 to 3, never falling along the last dimension, each value on 1 to 1024 neighbouring positions
- first_gain: bfloat16 [2048], replicated, may hold values from 0.5 to 1.5
- first_shift: bfloat16 [2048], replicated, may hold values from -3 to 3
- second_gain: bfloat16 [2048], replicated, may hold values from 0.5 to 1.5
- second_shift: bfloat16 [2048], replicated, may hold values from -3 to 3
- qkv_weight: bfloat16 [2048, 8, 768], P('dp', 'tensor'), may hold values from -0.125 to 0.125
- qkv_bias: bfloat16 [8, 768], P('tensor'), may hold values from -3 to 3
- out_weight: bfloat16 [2048, 2048], P('tensor', 'dp'), may hold values from -1 to 1
- out_bias: bfloat16 [2048], replicated, may hold values from -3 to 3
- up_projection_weight: bfloat16 [2048, 8192], P('dp', 'tensor'), may hold values from -0.125 to 0.125
- up_bias: bfloat16 [8192], P('tensor'), may hold values from -3 to 3
- down_weight: bfloat16 [8192, 2048], P('tensor', 'dp'), may hold values from -0.0625 to 0.0625
- down_bias: bfloat16 [2048], replicated, may hold values from -3 to 3
- cotangent: bfloat16 [8192, 2048], P(('dp', 'tensor')), may hold values from -6 to 6
Outputs:
- output: bfloat16 [8192, 2048], P(('dp', 'tensor'))
- layer_input_gradient: float32 [8192, 2048], P(('dp', 'tensor'))
- first_gain_grad: float32 [2048], replicated
- first_shift_grad: float32 [2048], replicated
- second_gain_grad: float32 [2048], replicated
- second_shift_grad: float32 [2048], replicated
- qkv_weight_grad: float32 [2048, 8, 768], P('dp', 'tensor')
- qkv_bias_grad: float32 [8, 768], P('tensor')
- out_weight_grad: float32 [2048, 2048], P('tensor', 'dp')
- out_bias_grad: float32 [2048], replicated
- up_weight_grad: float32 [2048, 8192], P('dp', 'tensor')
- up_bias_grad: float32 [8192], P('tensor')
- down_weight_grad: float32 [8192, 2048], P('tensor', 'dp')
- down_bias_grad: float32 [2048], replicated
Inputs may be any that keep to these rules, and one draw needn't show every extreme that they name: `segment_ids`: within each group the segment numbers never fall; each sequence has 1 to 1024 tokens and one of them exactly 1024; every number up to the largest occurs.
All inputs are finite; a program needn't handle non-finite values.
Results may differ from a plain program's by a relative error of at most 0.014.
Values may be sent and summed in bfloat16 or wider, within the bound.
No kernel may reach another device: no remote copies, remote signals or barrier semaphores. Data moves between devices by JAX's collectives and lax.ppermute only.
A program may use at most 192 MiB of HBM per device.

v0:
```python
from functools import partial
import math
import jax
import jax.numpy as jnp
from jax import lax
from jax.sharding import PartitionSpec as P

HD = 256
ROT = 64
NORM_EPS = 1e-05
MASK_FILL = -1e30


def normalize(values):
    mean_val = jnp.mean(values, axis=-1, keepdims=True)
    centred = values - mean_val
    spread = jnp.mean(centred * centred, axis=-1, keepdims=True)
    inv_std = lax.rsqrt(spread + NORM_EPS)
    return (centred * inv_std, inv_std)


def positions_of(segment):
    row_count = segment.shape[0]
    position_index = jnp.arange(row_count, dtype=jnp.int32)
    starts = jnp.concatenate([jnp.ones((1,), dtype=jnp.bool_), segment[1:] != segment[:-1]])
    first_index = lax.cummax(
        jnp.where(starts, position_index, jnp.zeros_like(position_index)), axis=0
    )
    return position_index - first_index


def rotation_tables(position):
    half_dims = ROT // 2
    inv_freq = 10000.0 ** (-2.0 * jnp.arange(half_dims, dtype=jnp.float32) / ROT)
    angles = position.astype(jnp.float32)[:, None] * inv_freq[None, :]
    return (jnp.cos(angles), jnp.sin(angles))


def rotate(values, cosine_table, sine_table, direction):
    half_dims = ROT // 2
    leading = values[:, :half_dims]
    trailing = values[:, half_dims:ROT]
    return jnp.concatenate(
        [
            leading * cosine_table - direction * trailing * sine_table,
            trailing * cosine_table + direction * leading * sine_table,
            values[:, ROT:],
        ],
        axis=1,
    )


def body(
    tokens,
    segment_ids,
    first_gain,
    first_shift,
    second_gain,
    second_shift,
    qkv_weight,
    qkv_bias,
    out_weight,
    out_bias,
    up_projection_weight,
    up_bias,
    down_weight,
    down_bias,
    cotangent,
):
    width = tokens.shape[1]
    heads_here = qkv_weight.shape[1]
    qkv_cols = heads_here * 3 * HD
    attn_cols = heads_here * HD
    segment = segment_ids[0]
    group_rows = segment.shape[0]
    block_rows = min(512, group_rows)
    block_count = group_rows // block_rows
    position = positions_of(segment)
    cosine_table, sine_table = rotation_tables(position)
    position_index = jnp.arange(group_rows, dtype=jnp.int32)
    score_scale = 1.0 / math.sqrt(HD)
    x_values = tokens.astype(jnp.float32)
    normed, inv_std = normalize(x_values)
    first_gain_f = first_gain.astype(jnp.float32)
    second_gain_f = second_gain.astype(jnp.float32)
    normed_local = normed.astype(jnp.bfloat16)
    normed_all = lax.all_gather(normed_local, "tensor", axis=0, tiled=True).astype(jnp.float32)
    first_all = (normed_all * first_gain_f + first_shift.astype(jnp.float32)).astype(jnp.bfloat16)
    second_all = (normed_all * second_gain_f + second_shift.astype(jnp.float32)).astype(
        jnp.bfloat16
    )
    joined_in = jnp.concatenate(
        [qkv_weight.reshape(qkv_weight.shape[0], qkv_cols), up_projection_weight], axis=1
    )
    joined_out = jnp.concatenate([out_weight, down_weight], axis=0)
    weight_piece = lax.all_gather(joined_in, "dp", axis=0, tiled=True)
    left_cols = first_all
    right_cols = second_all
    proj = jnp.dot(left_cols, weight_piece[:, :qkv_cols], preferred_element_type=jnp.float32)
    up_preactivation = jnp.dot(
        right_cols, weight_piece[:, qkv_cols:], preferred_element_type=jnp.float32
    )
    proj = proj.reshape(group_rows, heads_here, 3 * HD) + qkv_bias.astype(jnp.float32)[None]
    up_preactivation = up_preactivation + up_bias.astype(jnp.float32)[None]
    query_heads, key_heads, value_heads = ([], [], [])
    head_index = 0
    head_proj = proj[:, head_index]
    query_heads.append(
        rotate(head_proj[:, :HD], cosine_table, sine_table, 1.0).astype(jnp.bfloat16)
    )
    key_heads.append(
        rotate(head_proj[:, HD : 2 * HD], cosine_table, sine_table, 1.0).astype(jnp.bfloat16)
    )
    value_heads.append(head_proj[:, 2 * HD :].astype(jnp.bfloat16))

    def block_scores(query_block, key_rows, row_start, key_count):
        raw = (
            jnp.einsum("qd,kd->qk", query_block, key_rows, preferred_element_type=jnp.float32)
            * score_scale
        )
        seg_query = segment[row_start : row_start + block_rows]
        allowed = (seg_query[:, None] == segment[None, :key_count]) & (
            position_index[row_start : row_start + block_rows, None]
            >= position_index[None, :key_count]
        )
        return jnp.where(allowed, raw, MASK_FILL)

    attn_heads, lse_heads = ([], [])
    head_index = 0
    rows_out = []
    lse_rows = []
    for block_index in range(block_count):
        row_start = block_index * block_rows
        key_count = row_start + block_rows
        scores = block_scores(
            query_heads[head_index][row_start:key_count],
            key_heads[head_index][:key_count],
            row_start,
            key_count,
        )
        row_top = jnp.max(scores, axis=1, keepdims=True)
        exp_scores = jnp.exp(scores - row_top)
        row_total = jnp.sum(exp_scores, axis=1, keepdims=True)
        probs_low = (exp_scores / row_total).astype(jnp.bfloat16)
        rows_out.append(
            jnp.dot(
                probs_low, value_heads[head_index][:key_count], preferred_element_type=jnp.float32
            ).astype(jnp.bfloat16)
        )
        lse_rows.append(row_top + jnp.log(row_total))
    attn_heads.append(jnp.concatenate(rows_out, axis=0))
    lse_heads.append(jnp.concatenate(lse_rows, axis=0))
    attn = attn_heads[0]
    act = jax.nn.gelu(up_preactivation, approximate=False).astype(jnp.bfloat16)
    mixed = jnp.concatenate([attn, act], axis=1)
    incomplete_sum = jnp.dot(
        mixed,
        lax.all_gather(joined_out, "dp", axis=1, tiled=True),
        preferred_element_type=jnp.float32,
    )
    summed = lax.psum_scatter(
        incomplete_sum.astype(jnp.bfloat16), "tensor", scatter_dimension=0, tiled=True
    ).astype(jnp.float32)
    output = (
        x_values + out_bias.astype(jnp.float32) + down_bias.astype(jnp.float32) + summed
    ).astype(jnp.bfloat16)
    cot_all = lax.all_gather(cotangent, "tensor", axis=0, tiled=True)
    cot_cols = cot_all
    back_mixed = jnp.einsum(
        "gd,fd->gf",
        cot_cols,
        lax.all_gather(joined_out, "dp", axis=1, tiled=True),
        preferred_element_type=jnp.float32,
    )
    d_attn = back_mixed[:, :attn_cols].astype(jnp.bfloat16)
    gelu_pull = jax.vjp(partial(jax.nn.gelu, approximate=False), up_preactivation)[1]
    d_up = gelu_pull(back_mixed[:, attn_cols:])[0].astype(jnp.bfloat16)
    head_index = 0
    query_grads = []
    key_grad = jnp.zeros((group_rows, HD), jnp.float32)
    value_grad = jnp.zeros((group_rows, HD), jnp.float32)
    for block_index in range(block_count):
        row_start = block_index * block_rows
        key_count = row_start + block_rows
        query_block = query_heads[head_index][row_start:key_count]
        key_rows = key_heads[head_index][:key_count]
        scores = block_scores(query_block, key_rows, row_start, key_count)
        probs = jnp.exp(scores - lse_heads[head_index][row_start:key_count])
        grad_block = d_attn[row_start:key_count]
        d_probs = jnp.einsum(
            "qd,kd->qk",
            grad_block,
            value_heads[head_index][:key_count],
            preferred_element_type=jnp.float32,
        )
        d_scores = (probs * (d_probs - jnp.sum(probs * d_probs, axis=1, keepdims=True))).astype(
            jnp.bfloat16
        )
        query_grads.append(
            jnp.dot(d_scores, key_rows, preferred_element_type=jnp.float32) * score_scale
        )
        key_grad = key_grad.at[:key_count].add(
            jnp.einsum("qk,qd->kd", d_scores, query_block, preferred_element_type=jnp.float32)
            * score_scale
        )
        value_grad = value_grad.at[:key_count].add(
            jnp.einsum(
                "qk,qd->kd",
                probs.astype(jnp.bfloat16),
                grad_block,
                preferred_element_type=jnp.float32,
            )
        )
    query_grad = rotate(jnp.concatenate(query_grads, axis=0), cosine_table, sine_table, -1.0)
    key_grad = rotate(key_grad, cosine_table, sine_table, -1.0)
    d_proj_heads = jnp.concatenate([query_grad, key_grad, value_grad], axis=1)
    d_proj = d_proj_heads.astype(jnp.bfloat16)
    qkv_bias_part = jnp.sum(d_proj, axis=0, dtype=jnp.float32).reshape(heads_here, 3 * HD)
    up_bias_part = jnp.sum(d_up, axis=0, dtype=jnp.float32)
    qkv_bias_grad, up_bias_grad = lax.psum((qkv_bias_part, up_bias_part), "dp")
    weight_piece = lax.all_gather(joined_in, "dp", axis=0, tiled=True)
    d_hidden = jnp.stack(
        (
            jnp.einsum(
                "gf,df->gd", d_proj, weight_piece[:, :qkv_cols], preferred_element_type=jnp.float32
            ),
            jnp.einsum(
                "gf,df->gd", d_up, weight_piece[:, qkv_cols:], preferred_element_type=jnp.float32
            ),
        )
    )
    d_first_part = d_hidden[0]
    d_second_part = d_hidden[1]
    grad_part = d_first_part * first_gain_f + d_second_part * second_gain_f
    grad_normed = lax.psum_scatter(
        grad_part.astype(jnp.bfloat16), "tensor", scatter_dimension=0, tiled=True
    ).astype(jnp.float32)
    shard_rows = width // lax.axis_size("dp")
    left_cols = first_all
    right_cols = second_all
    in_grad = lax.psum_scatter(
        jnp.concatenate(
            [
                jnp.einsum("gd,gf->df", left_cols, d_proj, preferred_element_type=jnp.float32),
                jnp.einsum("gd,gf->df", right_cols, d_up, preferred_element_type=jnp.float32),
            ],
            axis=1,
        ).astype(jnp.bfloat16),
        "dp",
        scatter_dimension=0,
        tiled=True,
    ).astype(jnp.float32)
    qkv_weight_grad = in_grad[:, :qkv_cols].reshape(shard_rows, heads_here, 3 * HD)
    up_weight_grad = in_grad[:, qkv_cols:]
    cot_cols = cot_all
    out_grad = (
        lax.psum_scatter(
            jnp.einsum("gd,gf->df", cot_cols, mixed, preferred_element_type=jnp.float32).astype(
                jnp.bfloat16
            ),
            "dp",
            scatter_dimension=0,
            tiled=True,
        )
        .astype(jnp.float32)
        .T
    )
    out_weight_grad = out_grad[:attn_cols]
    down_weight_grad = out_grad[attn_cols:]
    cot_values = cotangent.astype(jnp.float32)
    stat_terms = (
        jnp.sum(d_first_part * normed_all, axis=0),
        jnp.sum(d_first_part, axis=0),
        jnp.sum(d_second_part * normed_all, axis=0),
        jnp.sum(d_second_part, axis=0),
        jnp.sum(cot_values, axis=0),
    )
    first_gain_grad, first_shift_grad, second_gain_grad, second_shift_grad, bias_grad = lax.psum(
        (stat_terms[0], stat_terms[1], stat_terms[2], stat_terms[3], stat_terms[4]),
        ("dp", "tensor"),
    )
    layer_input_gradient = cot_values + inv_std * (
        grad_normed
        - jnp.mean(grad_normed, axis=1, keepdims=True)
        - normed * jnp.mean(grad_normed * normed, axis=1, keepdims=True)
    )
    return (
        output,
        layer_input_gradient,
        first_gain_grad,
        first_shift_grad,
        second_gain_grad,
        second_shift_grad,
        qkv_weight_grad,
        qkv_bias_grad,
        out_weight_grad,
        bias_grad,
        up_weight_grad,
        up_bias_grad,
        down_weight_grad,
        bias_grad,
    )


def solution(mesh):
    return jax.shard_map(
        body,
        mesh=mesh,
        in_specs=(
            P(("dp", "tensor"), None),
            P("dp", None),
            P(),
            P(),
            P(),
            P(),
            P("dp", "tensor", None),
            P("tensor", None),
            P("tensor", "dp"),
            P(),
            P("dp", "tensor"),
            P("tensor"),
            P("tensor", "dp"),
            P(),
            P(("dp", "tensor"), None),
        ),
        out_specs=(
            P(("dp", "tensor"), None),
            P(("dp", "tensor"), None),
            P(),
            P(),
            P(),
            P(),
            P("dp", "tensor", None),
            P("tensor", None),
            P("tensor", "dp"),
            P(),
            P("dp", "tensor"),
            P("tensor"),
            P("tensor", "dp"),
            P(),
        ),
        check_vma=False,
    )
```

profile of v0, /device:TPU:0, one launch (start us, length us, event | category | flops | bytes accessed | tf_op | source)
XLA Modules:
  0.0 931.8 jit_solution(4971245081132490845)
XLA Ops:
  7.2 2.9 pad_maximum_fusion.3
  11.0 1.3 fusion.50
  15.2 50.1 %all-gather.7.cloned.1.call-done = bf16[2048,1792]{1,0:T(8,128)(2,1)} async-done(((bf16[512,1792]{1,0:T(8,128)(2,1)}), bf16[2048,1792]{1,0:T(8,128)(2,1)}) %all-gather.7.cloned.1.call-update) | async-done | bytes 7340048 | tf_op jit(solution)/shard_map/all_gather | solution.py:96
  65.3 127.7 %all-gather.5.cloned.1.call-done = bf16[2048,2048]{1,0:T(8,128)(2,1)} async-done(((bf16[256,2048]{1,0:T(8,128)(2,1)}), bf16[2048,2048]{1,0:T(8,128)(2,1)}) %all-gather.5.cloned.1.call-update) | async-done | bytes 8388624 | tf_op jit(solution)/shard_map/all_gather | solution.py:87
  193.0 10.5 %fusion.156 = (bf16[2048,768]{0,1:T(8,128)(2,1)S(1)}, f32[2048,768]{0,1:T(8,128)S(1)}) fusion(f32[768]{0:T(1024)S(1)} %convert_reduce_fusion.5, bf16[2048,1792]{1,0:T(8,128)(2,1)} %all-gather.7.cloned.1.call-done, bf16[2048,2048]{1,0:T(8,128)(2,1)} %all-gather.5.cloned.1.call-done, f32[2048]{0:T(1024)S(1)} %convert_element_type.144, ...), kind=kOutput, calls=%fused_computation.244 | convolution fusion | flops 6462373888 | bytes 20990976 | tf_op jit(solution)/shard_map/dot_general | solution.py:99
  203.5 1.5 fusion.116
  209.2 1.4 fusion.158
  211.3 1.3 convolution_convert_fusion.3
  213.9 1.4 fusion.71
  215.3 1.6 fusion.72
  216.9 16.8 %all-gather.9.cloned.1.call-done = bf16[1280,2048]{1,0:T(8,128)(2,1)} async-done(((bf16[1280,512]{1,0:T(8,128)(2,1)}), bf16[1280,2048]{1,0:T(8,128)(2,1)}) %all-gather.9.cloned.1.call-update) | async-done | bytes 5242896 | tf_op jit(solution)/shard_map/all_gather | solution.py:158
  233.8 126.9 %all-gather.11.cloned.1.call-done = bf16[2048,2048]{1,0:T(8,128)(2,1)} async-done(((bf16[256,2048]{1,0:T(8,128)(2,1)}), bf16[2048,2048]{1,0:T(8,128)(2,1)}) %all-gather.11.cloned.1.call-update) | async-done | bytes 8388624 | tf_op jit(solution)/shard_map/all_gather | solution.py:167
  360.7 17.3 %fusion.157 = (bf16[2048,1280]{1,0:T(8,128)(2,1)S(1)}, f32[2048,1280]{1,0:T(8,128)}) fusion(bf16[1280,2048]{1,0:T(8,128)(2,1)} %all-gather.9.cloned.1.call-done, bf16[2048,2048]{1,0:T(8,128)(2,1)} %all-gather.11.cloned.1.call-done), kind=kOutput, calls=%fused_computation.245 | convolution fusion | flops 10740039680 | bytes 29360128 | tf_op jit(solution)/shard_map/gd,fd->gf/dot_general | solution.py:169
  379.1 2.6 convolution_multiply_fusion.9
  381.8 1.6 scatter-add.20
  383.4 1.5 scatter-add.25
  386.1 1.3 convolution_multiply_fusion.6
  389.1 1.4 convolution_multiply_fusion.7
  393.7 1.5 convolution_multiply_fusion.5
  395.9 33.3 %convert_reduce_fusion = (f32[1024]{0:T(1024)S(1)}, bf16[2048,1024]{1,0:T(8,128)(2,1)}, f32[2048,1024]{1,0:T(8,128)}, f32[2048,1024]{1,0:T(8,128)}) fusion(f32[2048,1280]{1,0:T(8,128)} %get-tuple-element.190, f32[1024]{0:T(1024)S(1)} %convert_element_type.158, bf16[2048,1792]{1,0:T(8,128)(2,1)} %all-gather.7.cloned.1.call-done, ...), kind=kOutput, calls=%fused_computation.14 | convolution fusion | flops 8763997184 | bytes 41967616 | tf_op jit(solution)/shard_map/dot_general | solution.py:100
  429.2 10.2 %multiply_convert_fusion = bf16[2048,1024]{1,0:T(8,128)(2,1)} fusion(f32[2048,1024]{1,0:T(8,128)} %get-tuple-element.169, f32[2048,1024]{1,0:T(8,128)} %get-tuple-element.186, f32[1024]{0:T(1024)S(1)} %convert_element_type.158), kind=kLoop, calls=%fused_computation.16 | loop fusion | flops 8388608 | bytes 20975616 | tf_op jit(solution)/shard_map/convert_element_type | solution.py:154
  439.5 16.7 %fusion.12 = bf16[2048,1280]{0,1:T(8,128)(2,1)} fusion(bf16[2048,2048]{1,0:T(8,128)(2,1)} %all-gather.11.cloned.1.call-done, bf16[2048,1024]{1,0:T(8,128)(2,1)} %multiply_convert_fusion, bf16[512,256]{1,0:T(8,128)(2,1)S(1)} %copy-done.60, bf16[512,256]{1,0:T(8,128)(2,1)S(1)} %copy-done.58, bf16[512,256]{1,0:T(8,128)(2,1)S(1)} %copy-done.57, ...), kind=kOutput, calls=%fused_computation.33 | convolution fusion | flops 10766254080 | bytes 18874368 | tf_op jit(solution)/shard_map/gd,gf->df/dot_general | solution.py:258
  457.1 1.5 convolution_multiply_fusion.8
  458.6 2.8 pad_maximum_fusion.2
  461.4 2.4 fusion.68
  463.8 1.9 fusion.69
  467.3 2.1 fusion.39
  469.4 1.5 fusion.149
  474.7 2.0 fusion.46
  476.7 8.2 fusion.30
  484.9 10.1 %fusion.22 = bf16[2048,1024]{0,1:T(8,128)(2,1)S(1)} fusion(bf16[2048,1024]{1,0:T(8,128)(2,1)S(1)} %copy-done.59, bf16[2048,2048]{1,0:T(8,128)(2,1)S(1)} %bitcast.51, f32[2048]{0:T(1024)S(1)} %convert_element_type.156, f32[2048]{0:T(1024)S(1)} %convert_element_type.155), kind=kOutput, calls=%fused_computation.48 | convolution fusion | flops 8608808960 | bytes 16793600 | tf_op jit(solution)/shard_map/gd,gf->df/dot_general | solution.py:245
  495.0 5.9 pad_maximum_fusion
  501.0 1.8 copy-done.26
  502.8 13.0 %fusion.41 = f32[2048,2048]{1,0:T(8,128)} fusion(bf16[2048,768]{0,1:T(8,128)(2,1)S(1)} %copy-done.26, bf16[2048,1792]{1,0:T(8,128)(2,1)} %all-gather.7.cloned.1.call-done), kind=kOutput, calls=%fused_computation.75 | convolution fusion | flops 6442450944 | bytes 23068672 | tf_op jit(solution)/shard_map/gf,df->gd/dot_general | solution.py:224
  515.8 25.9 %fusion.151 = (f32[2048]{0:T(1024)S(1)}, f32[2048]{0:T(1024)S(1)}, bf16[2048,2048]{1,0:T(8,128)(2,1)}, f32[2048]{0:T(1024)S(1)}, f32[2048]{0:T(1024)S(1)}) fusion(bf16[2048,2048]{1,0:T(8,128)(2,1)} %all-gather.5.cloned.1.call-done, f32[2048]{0:T(1024)S(1)} %convert_element_type.155, f32[2048,2048]{1,0:T(8,128)} %fusion.41, f32[2048]{0:T(1024)S(1)} %copy-done.44, ...), kind=kOutput, calls=%fused_computation.240 | convolution fusion | flops 8636063744 | bytes 41992192 | tf_op jit(solution)/shard_map/gf,df->gd/dot_general | solution.py:227
  541.8 17.4 %convolution_convert_fusion = bf16[2048,2048]{1,0:T(8,128)(2,1)} fusion(bf16[1280,2048]{1,0:T(8,128)(2,1)} %all-gather.9.cloned.1.call-done, bf16[2048,1024]{1,0:T(8,128)(2,1)} %multiply_convert_fusion, bf16[512,256]{1,0:T(8,128)(2,1)} %fusion.72, bf16[512,256]{1,0:T(8,128)(2,1)} %fusion.71, bf16[512,256]{1,0:T(8,128)(2,1)} %convolution_convert_fusion.2, ...), kind=kOutput, calls=%fused_computation.30 | convolution fusion | flops 10767826944 | bytes 18874368 | tf_op jit(solution)/shard_map/dot_general | solution.py:156
  560.4 7.0 all-reduce.3
  567.4 1.7 convert_bitcast_fusion
  569.9 1.5 slice.435
  571.4 2.8 reduce-scatter.9.cloned.1.call-done
  574.2 3.0 slice.434
  577.2 2.9 copy.42
  580.7 2.8 copy.41
  583.5 143.4 %reduce-scatter.7.cloned.1.call-done = bf16[256,2048]{1,0:T(8,128)(2,1)} async-done(((bf16[2048,2048]{1,0:T(8,128)(2,1)}), bf16[256,2048]{1,0:T(8,128)(2,1)}) %reduce-scatter.7.cloned.1.call-update) | async-done | bytes 1048592 | tf_op jit(solution)/shard_map/reduce_scatter | solution.py:235
  726.9 1.9 convert_reduce_fusion.2
  728.8 150.1 %reduce-scatter.5.cloned.1.call-done = bf16[256,2048]{1,0:T(8,128)(2,1)} async-done(((bf16[2048,2048]{1,0:T(8,128)(2,1)}), bf16[256,2048]{1,0:T(8,128)(2,1)}) %reduce-scatter.5.cloned.1.call-update) | async-done | bytes 1048592 | tf_op jit(solution)/shard_map/reduce_scatter | solution.py:161
  879.0 4.9 convert_reduce_fusion.4
  883.8 40.3 %all-reduce.2 = (f32[2048]{0:T(1024)}, f32[2048]{0:T(1024)}, f32[2048]{0:T(1024)}, f32[2048]{0:T(1024)}, f32[2048]{0:T(1024)S(1)}) all-reduce(f32[2048]{0:T(1024)S(1)} %get-tuple-element.171, f32[2048]{0:T(1024)S(1)} %get-tuple-element.172, f32[2048]{0:T(1024)S(1)} %get-tuple-element.155, ...), channel_id=1, replica_groups=mesh['dp'=4,'tensor'=8] {'dp','tensor'}, use_global_device_ids=true, to_apply=%region_21.22 | all-reduce | flops 10240 | bytes 81920 | tf_op jit(solution)/shard_map/psum | solution.py:278
  (218 shorter events, 26.7 us)
Async XLA Ops:
  7.2 58.1 %all-gather.7.cloned.1.call-start = ((), (), s32[]{:S(2)}) async-start(), calls=%async_computation.5 | async-start | bytes 9175040 | tf_op jit(solution)/shard_map/all_gather | solution.py:96
  10.1 182.8 %all-gather.5.cloned.1.call-start = ((), (), s32[]{:S(2)}) async-start(), calls=%async_computation.4 | async-start | bytes 9437184 | tf_op jit(solution)/shard_map/all_gather | solution.py:87
  10.4 3.7 copy-start.37
  10.9 3.4 copy-start.36
  10.9 4.2 copy-start.54
  11.0 192.5 %copy-start.39 = (f32[256]{0:T(256)}, f32[256]{0:T(256)S(1)}, u32[]{:S(2)}) copy-start(f32[256]{0:T(256)S(1)} %add_rsqrt_fusion) | copy-start | bytes 3076
  12.3 221.5 %all-gather.9.cloned.1.call-start = ((), (), s32[]{:S(2)}) async-start(), calls=%async_computation.6 | async-start | bytes 6553600 | tf_op jit(solution)/shard_map/all_gather | solution.py:158
  13.5 347.2 %all-gather.11.cloned.1.call-start = ((), (), s32[]{:S(2)}) async-start(), calls=%async_computation.8 | async-start | bytes 9437184 | tf_op jit(solution)/shard_map/all_gather | solution.py:167
  14.1 553.3 %reduce-scatter.11.cloned.1.call-start = ((), (), s32[]{:S(2)}) async-start(), calls=%async_computation.11 | async-start | bytes 6553600 | tf_op jit(solution)/shard_map/reduce_scatter | solution.py:257
  14.2 189.3 %copy-start.43 = (f32[2048]{0:T(1024)}, f32[2048]{0:T(1024)S(1)}, u32[]{:S(2)}) copy-start(f32[2048]{0:T(1024)S(1)} %convert_element_type.143) | copy-start | bytes 24580
  14.3 189.3 %copy-start.45 = (f32[2048]{0:T(1024)}, f32[2048]{0:T(1024)S(1)}, u32[]{:S(2)}) copy-start(f32[2048]{0:T(1024)S(1)} %convert_element_type.144) | copy-start | bytes 24580
  14.9 188.6 %copy-start.41 = (f32[32]{0:T(128)}, f32[32]{0:T(128)S(1)}, u32[]{:S(2)}) copy-start(f32[32]{0:T(128)S(1)} %multiply_power_fusion) | copy-start | bytes 388
  15.2 188.3 %copy-start.33 = (f32[2048]{0:T(1024)}, f32[2048]{0:T(1024)S(1)}, u32[]{:S(2)}) copy-start(f32[2048]{0:T(1024)S(1)} %fusion.150) | copy-start | bytes 24580
  203.5 11.8 %copy-start.19 = (bf16[2048,768]{0,1:T(8,128)(2,1)}, bf16[2048,768]{0,1:T(8,128)(2,1)S(1)}, u32[]{:S(2)}) copy-start(bf16[2048,768]{0,1:T(8,128)(2,1)S(1)} %get-tuple-element.187) | copy-start | bytes 9437188
  205.2 3.9 copy-start.15
  205.6 3.6 copy-start.22
  206.0 5.3 copy-start.10
  207.0 5.7 copy-start.3
  210.6 4.8 copy-start
  360.7 17.3 %copy-start.11 = (f32[512,512]{0,1:T(8,128)S(1)}, f32[512,512]{0,1:T(8,128)}, u32[]{:S(2)}) copy-start(f32[512,512]{0,1:T(8,128)} %copy-done.10) | copy-start | bytes 3145732
  360.7 17.7 %copy-start.20 = (bf16[2048,768]{0,1:T(8,128)(2,1)S(1)}, bf16[2048,768]{0,1:T(8,128)(2,1)}, u32[]{:S(2)}) copy-start(bf16[2048,768]{0,1:T(8,128)(2,1)} %copy-done.19) | copy-start | bytes 9437188
  378.0 12.4 %copy-start.32 = (bf16[2048,1280]{1,0:T(8,128)(2,1)}, bf16[2048,1280]{1,0:T(8,128)(2,1)S(1)}, u32[]{:S(2)}) copy-start(bf16[2048,1280]{1,0:T(8,128)(2,1)S(1)} %get-tuple-element.189) | copy-start | bytes 15728644
  378.8 6.1 copy-start.4
  379.1 6.4 copy-start.21
  391.3 3.9 slice-start.1
  392.4 3.5 slice-start.2
  393.7 35.5 %copy-start.13 = (bf16[512,2048]{1,0:T(8,128)(2,1)}, bf16[512,2048]{1,0:T(8,128)(2,1)S(1)}, u32[]{:S(2)}) copy-start(bf16[512,2048]{1,0:T(8,128)(2,1)S(1)} %multiply_convert_fusion.1) | copy-start | bytes 6291460
  429.2 10.2 %copy-start.56 = (bf16[512,256]{1,0:T(8,128)(2,1)S(1)}, bf16[512,256]{1,0:T(8,128)(2,1)}, u32[]{:S(2)}) copy-start(bf16[512,256]{1,0:T(8,128)(2,1)} %convolution_convert_fusion.3) | copy-start | bytes 786436
  429.2 10.2 %copy-start.57 = (bf16[512,256]{1,0:T(8,128)(2,1)S(1)}, bf16[512,256]{1,0:T(8,128)(2,1)}, u32[]{:S(2)}) copy-start(bf16[512,256]{1,0:T(8,128)(2,1)} %convolution_convert_fusion.2) | copy-start | bytes 786436
  429.2 10.2 %copy-start.58 = (bf16[512,256]{1,0:T(8,128)(2,1)S(1)}, bf16[512,256]{1,0:T(8,128)(2,1)}, u32[]{:S(2)}) copy-start(bf16[512,256]{1,0:T(8,128)(2,1)} %fusion.71) | copy-start | bytes 786436
  429.2 10.2 %copy-start.60 = (bf16[512,256]{1,0:T(8,128)(2,1)S(1)}, bf16[512,256]{1,0:T(8,128)(2,1)}, u32[]{:S(2)}) copy-start(bf16[512,256]{1,0:T(8,128)(2,1)} %fusion.72) | copy-start | bytes 786436
  456.2 118.0 %reduce-scatter.9.cloned.1.call-start = ((), (), s32[]{:S(2)}) async-start(), calls=%async_computation.10 | async-start | bytes 9175040 | tf_op jit(solution)/shard_map/reduce_scatter | solution.py:241
  457.1 4.3 copy-start.8
  457.1 6.7 copy-start.5
  457.1 6.7 copy-start.9
  461.4 4.4 copy-start.18
  461.4 4.4 copy-start.23
  467.3 9.4 %slice-start.3 = ((s8[8388608]{0:T(1024)(128)(4,1)}), s8[4194304]{0:T(1024)(128)(4,1)S(1)}, s32[]{:S(2)}) async-start(s8[8388608]{0:T(1024)(128)(4,1)} %bitcast.50), calls=%async_computation.15 | async-start | bytes 8388608
  469.4 5.2 copy-start.2
  472.3 4.4 slice-start.4
  476.7 8.2 copy-start.25
  476.7 8.2 copy-start.59
  500.9 226.0 %reduce-scatter.7.cloned.1.call-start = ((), (), s32[]{:S(2)}) async-start(), calls=%async_computation.9 | async-start | bytes 9437184 | tf_op jit(solution)/shard_map/reduce_scatter | solution.py:235
  541.8 337.2 %reduce-scatter.5.cloned.1.call-start = ((), (), s32[]{:S(2)}) async-start(), calls=%async_computation.7 | async-start | bytes 9437184 | tf_op jit(solution)/shard_map/reduce_scatter | solution.py:161
  574.2 5.9 copy-start.12
  580.6 146.3 %copy-start.7 = (bf16[256,2048]{1,0:T(8,128)(2,1)S(1)}, bf16[256,2048]{1,0:T(8,128)(2,1)}, u32[]{:S(2)}) copy-start(bf16[256,2048]{1,0:T(8,128)(2,1)} %param.35) | copy-start | bytes 3145732
  580.6 146.3 %copy-start.38 = (f32[256]{0:T(256)S(1)}, f32[256]{0:T(256)}, u32[]{:S(2)}) copy-start(f32[256]{0:T(256)} %copy-done.37) | copy-start | bytes 3076
  580.6 146.3 %copy-start.40 = (f32[256]{0:T(256)S(1)}, f32[256]{0:T(256)}, u32[]{:S(2)}) copy-start(f32[256]{0:T(256)} %copy-done.39) | copy-start | bytes 3076
  (26 other events, 55.3 us)
Sparse Core Ops, SparseCore 0:
  10.3 55.0 all-gather.6
  68.0 124.9 all-gather.4
  195.1 38.6 all-gather.8
  235.8 124.9 all-gather.10
  456.3 49.5 reduce-scatter.10
  508.5 65.6 reduce-scatter.8
  577.8 149.0 reduce-scatter.6
  731.0 147.9 reduce-scatter.4
where the time goes:
time: 937 us; the launch traced here: 932 us
  waiting for transfers between devices  619 us (66%)
  matrix products  183 us (20%)
  blocking collectives  47.3 us (5%)
  other arithmetic  46.1 us (5%)
  local copies, waits for them, and re-layouts  20.9 us (2%)
  between operations  15.5 us (2%)
    reduce_scatter x1, waiting for transfers between devices, body(): lax.psum_scatter(incomplete_sum.astype(jnp.bfloat16), 'tensor', scatter_d...  150 us
    reduce_scatter x1, waiting for transfers between devices, body(): lax.psum_scatter(grad_part.astype(jnp.bfloat16), 'tensor', scatter_dimens...  143 us
    all_gather x1, waiting for transfers between devices, body(): lax.all_gather(normed_local, 'tensor', axis=0, tiled=True)  128 us
    all_gather x1, waiting for transfers between devices, body(): cot_all = lax.all_gather(cotangent, 'tensor', axis=0, tiled=True)  127 us
    all_gather x1, waiting for transfers between devices, body(): weight_piece = lax.all_gather(joined_in, 'dp', axis=0, tiled=True)  50.1 us
    psum x1, blocking collectives, body(): lax.psum((stat_terms[0], stat_terms[1], stat_terms[2], stat_terms[3], sta...  40.3 us
    dot_general x1, matrix products, body(): jnp.dot(right_cols, weight_piece[:, qkv_cols:], preferred_element_type=jn...  33.3 us
    dot_general x1, matrix products, body(): jnp.einsum('gf,df->gd', d_up, weight_piece[:, qkv_cols:], preferred_eleme...  25.9 us
  transfers between devices with their start and end apart: 8, of which 7 were waited for; matrix products, arithmetic and copies ran while one was open for 15% of the time, Pallas kernels for 0%

commit v1 on v0

--- a/solution.py
+++ b/solution.py
@@ -9,6 +9,28 @@
 ROT = 64
 NORM_EPS = 1e-05
 MASK_FILL = -1e30
+
+
+def joined_along(blocks, dim):
+    blocks = jnp.moveaxis(blocks, 0, dim)
+    dims = blocks.shape
+    return blocks.reshape(*dims[:dim], dims[dim] * dims[dim + 1], *dims[dim + 2 :])
+
+
+def ring_gather(value, axis, dim):
+    size = lax.axis_size(axis)
+    pairs = [(i, (i + 1) % size) for i in range(size)]
+    back = [(b, a) for a, b in pairs]
+    lower, upper = ([], [])
+    for hop in range(size - 1):
+        if hop % 2 == 0:
+            lower.append(lax.ppermute(lower[-1] if lower else value, axis, pairs))
+        else:
+            upper.append(lax.ppermute(upper[-1] if upper else value, axis, back))
+    blocks = jnp.stack([*lower[::-1], value, *upper])
+    shift = lax.axis_index(axis) - len(lower)
+    blocks = blocks[(jnp.arange(size) - shift) % size]
+    return joined_along(blocks, dim)
 
 
 def normalize(values):
@@ -84,7 +106,7 @@
     first_gain_f = first_gain.astype(jnp.float32)
     second_gain_f = second_gain.astype(jnp.float32)
     normed_local = normed.astype(jnp.bfloat16)
-    normed_all = lax.all_gather(normed_local, "tensor", axis=0, tiled=True).astype(jnp.float32)
+    normed_all = ring_gather(normed_local, "tensor", 0).astype(jnp.float32)
     first_all = (normed_all * first_gain_f + first_shift.astype(jnp.float32)).astype(jnp.bfloat16)
     second_all = (normed_all * second_gain_f + second_shift.astype(jnp.float32)).astype(
         jnp.bfloat16

time: 937 us -> 847 us (0.904)
  waiting for transfers between devices: 619 us -> 438 us
  starting transfers between devices: 0.33 us -> 56.1 us
  local copies, waits for them, and re-layouts: 20.9 us -> 43.8 us
  other arithmetic: 46.1 us -> 58.3 us
    all_gather x1 -> x0, waiting for transfers between devices: 128 us -> none  [body(): lax.all_gather(normed_local, 'tensor', axis=0, tiled=True)]
    ppermute x0 -> x7, waiting for transfers between devices: none -> 121 us  [the longest x4 118 us: ring_gather(): lower.append(lax.ppermute(lower[-1] if lower else value, axis, pairs))]
    all_gather x1, waiting for transfers between devices: 127 us -> 19.6 us  [body(): cot_all = lax.all_gather(cotangent, 'tensor', axis=0, tiled=True)]
    ppermute x0 -> x7, starting transfers between devices: none -> 55.8 us  [the longest x3 47.7 us: ring_gather(): upper.append(lax.ppermute(upper[-1] if upper else value, axis, back))]
    all_gather x1, waiting for transfers between devices: 50.1 us -> 0.01 us  [body(): weight_piece = lax.all_gather(joined_in, 'dp', axis=0, tiled=True)]
    all_gather x1, waiting for transfers between devices: 16.8 us -> 0.01 us  [body(): lax.all_gather(joined_out, 'dp', axis=1, tiled=True)]
    unnamed x135 -> x155, local copies, waits for them, and re-layouts: 12 us -> 25.6 us
    convert_element_type x0 -> x1, other arithmetic: none -> 11 us  [body(): (normed_all * first_gain_f + first_shift.astype(jnp.float32)).astype(jnp....]
  transfers between devices with their start and end apart: 8 -> 14, of which waited for: 7 -> 9; matrix products, arithmetic and copies ran while one was open for 15% -> 21% of each run, Pallas kernels for 0% -> 0%
where the time goes in v1:
time: 847 us; the launch traced here: 839 us
  waiting for transfers between devices  438 us (52%)
  matrix products  179 us (21%)
  other arithmetic  58.3 us (7%)
  starting transfers between devices  56.1 us (7%)
  blocking collectives  47.7 us (6%)
  local copies, waits for them, and re-layouts  43.8 us (5%)
  between operations  15.8 us (2%)
    reduce_scatter x1, waiting for transfers between devices, body(): lax.psum_scatter(incomplete_sum.astype(jnp.bfloat16), 'tensor', scatter_d...  150 us
    reduce_scatter x1, waiting for transfers between devices, body(): lax.psum_scatter(grad_part.astype(jnp.bfloat16), 'tensor', scatter_dimens...  143 us
    ppermute x4, waiting for transfers between devices, ring_gather(): lower.append(lax.ppermute(lower[-1] if lower else value, axis, pairs))  118 us
    ppermute x3, starting transfers between devices, ring_gather(): upper.append(lax.ppermute(upper[-1] if upper else value, axis, back))  47.7 us
    psum x1, blocking collectives, body(): lax.psum((stat_terms[0], stat_terms[1], stat_terms[2], stat_terms[3], sta...  40.3 us
    dot_general x1, matrix products, body(): jnp.dot(right_cols, weight_piece[:, qkv_cols:], preferred_element_type=jn...  33 us
    dot_general x1, matrix products, body(): jnp.einsum('gf,df->gd', d_up, weight_piece[:, qkv_cols:], preferred_eleme...  26.8 us
    unnamed x155, local copies, waits for them, and re-layouts  25.6 us
  transfers between devices with their start and end apart: 14, of which 9 were waited for; matrix products, arithmetic and copies ran while one was open for 21% of the time, Pallas kernels for 0%

profile of v1, /device:TPU:0, one launch (start us, length us, event | category | flops | bytes accessed | tf_op | source)
XLA Modules:
  0.0 839.0 jit_solution(5243840962900930906)
XLA Ops:
  7.3 2.9 pad_maximum_fusion.3
  12.6 3.0 collective-permute-start
  15.6 26.2 %collective-permute-done = bf16[256,2048]{1,0:T(8,128)(2,1)S(1)} collective-permute-done((bf16[256,2048]{1,0:T(8,128)(2,1)S(1)}, bf16[256,2048]{1,0:T(8,128)(2,1)S(1)}, u32[]{:S(2)}, u32[]{:S(2)}) %collective-permute-start) | collective-permute-done | bytes 1048608 | tf_op jit(solution)/shard_map/ppermute | solution.py:27
  41.8 4.7 collective-permute-start.4
  46.6 39.9 %collective-permute-done.1 = bf16[256,2048]{1,0:T(8,128)(2,1)} collective-permute-done((bf16[256,2048]{1,0:T(8,128)(2,1)S(1)}, bf16[256,2048]{1,0:T(8,128)(2,1)}, u32[]{:S(2)}, u32[]{:S(2)}) %collective-permute-start.1) | collective-permute-done | bytes 1048608 | tf_op jit(solution)/shard_map/ppermute | solution.py:27
  86.4 2.6 collective-permute-start.2
  89.4 23.0 %collective-permute-start.5 = (bf16[256,2048]{1,0:T(8,128)(2,1)}, bf16[256,2048]{1,0:T(8,128)(2,1)S(1)}, u32[]{:S(2)}, u32[]{:S(2)}) collective-permute-start(bf16[256,2048]{1,0:T(8,128)(2,1)} %collective-permute-done.4), channel_id=1, source_target_pairs={{1,0},{2,1},{3,2},{4,3},{5,4},{6,5},{7,6},{0,7},{9,8},{10,9},{11,1... | collective-permute-start | bytes 3145736 | tf_op jit(solution)/shard_map/ppermute | solution.py:29
  112.4 32.0 %collective-permute-done.2 = bf16[256,2048]{1,0:T(8,128)(2,1)} collective-permute-done((bf16[256,2048]{1,0:T(8,128)(2,1)}, bf16[256,2048]{1,0:T(8,128)(2,1)}, u32[]{:S(2)}, u32[]{:S(2)}) %collective-permute-start.2) | collective-permute-done | bytes 1048608 | tf_op jit(solution)/shard_map/ppermute | solution.py:27
  144.4 2.5 collective-permute-start.3
  147.7 3.9 collective-permute-done.5
  151.6 20.0 %collective-permute-start.6 = (bf16[256,2048]{1,0:T(8,128)(2,1)S(1)}, bf16[256,2048]{1,0:T(8,128)(2,1)S(1)}, u32[]{:S(2)}, u32[]{:S(2)}) collective-permute-start(bf16[256,2048]{1,0:T(8,128)(2,1)S(1)} %collective-permute-done.5), channel_id=1, source_target_pairs={{1,0},{2,1},{3,2},{4,3},{5,4},{6,5},{7,6},{0,7},{9,8},{10,9},{11,1... | collective-permute-start | bytes 3145736 | tf_op jit(solution)/shard_map/ppermute | solution.py:29
  171.6 19.4 %collective-permute-done.3 = bf16[256,2048]{1,0:T(8,128)(2,1)} collective-permute-done((bf16[256,2048]{1,0:T(8,128)(2,1)}, bf16[256,2048]{1,0:T(8,128)(2,1)}, u32[]{:S(2)}, u32[]{:S(2)}) %collective-permute-start.3) | collective-permute-done | bytes 1048608 | tf_op jit(solution)/shard_map/ppermute | solution.py:27
  191.0 2.3 bitcast_dynamic-update-slice_fusion.7
  193.3 2.6 bitcast_dynamic-update-slice_fusion.6
  195.9 2.3 bitcast_dynamic-update-slice_fusion.5
  200.6 2.3 bitcast_dynamic-update-slice_fusion.2
  205.1 8.1 gather_fusion
  213.2 11.0 %fusion.1 = (bf16[2048,2048]{1,0:T(8,128)(2,1)}, bf16[2048,2048]{1,0:T(8,128)(2,1)}) fusion(bf16[8,256,2048]{2,1,0:T(8,128)(2,1)} %gather_fusion, f32[2048]{0:T(1024)S(1)} %convert_element_type.148, f32[2048]{0:T(1024)S(1)} %convert_element_type.147, f32[2048]{0:T(1024)S(1)} %convert_element_type.160, f32[2048]{0:T(1024)S(1)} %convert_element_type.159), kind=kLoop, calls=%fused_computation.6 | loop fusion | flops 29360128 | bytes 25198592 | tf_op jit(solution)/shard_map/convert_element_type | solution.py:110
  224.2 10.4 %fusion.142 = (bf16[2048,768]{0,1:T(8,128)(2,1)S(1)}, f32[2048,768]{0,1:T(8,128)S(1)}) fusion(f32[768]{0:T(1024)S(1)} %convert_reduce_fusion.5, bf16[2048,2048]{1,0:T(8,128)(2,1)} %get-tuple-element.173, bf16[2048,1792]{1,0:T(8,128)(2,1)} %all-gather.4.cloned.1.call-done), kind=kOutput, calls=%fused_computation.257 | convolution fusion | flops 6445596672 | bytes 20974592 | tf_op jit(solution)/shard_map/dot_general | solution.py:121
  234.7 1.7 fusion.100
  247.4 19.6 %all-gather.8.cloned.1.call-done = bf16[2048,2048]{1,0:T(8,128)(2,1)} async-done(((bf16[256,2048]{1,0:T(8,128)(2,1)}), bf16[2048,2048]{1,0:T(8,128)(2,1)}) %all-gather.8.cloned.1.call-update) | async-done | bytes 8388624 | tf_op jit(solution)/shard_map/all_gather | solution.py:189
  267.0 17.0 %fusion.143 = (bf16[2048,1280]{1,0:T(8,128)(2,1)S(1)}, f32[2048,1280]{1,0:T(8,128)}) fusion(bf16[1280,2048]{1,0:T(8,128)(2,1)} %all-gather.6.cloned.1.call-done, bf16[2048,2048]{1,0:T(8,128)(2,1)} %all-gather.8.cloned.1.call-done), kind=kOutput, calls=%fused_computation.258 | convolution fusion | flops 10740039680 | bytes 29360128 | tf_op jit(solution)/shard_map/gd,fd->gf/dot_general | solution.py:191
  285.2 2.6 convolution_multiply_fusion.9
  297.3 3.0 multiply_reduce_fusion
  300.8 33.0 %convert_reduce_fusion = (f32[1024]{0:T(1024)S(1)}, bf16[2048,1024]{1,0:T(8,128)(2,1)}, f32[2048,1024]{1,0:T(8,128)}, f32[2048,1024]{1,0:T(8,128)}) fusion(f32[2048,1280]{1,0:T(8,128)} %get-tuple-element.192, f32[1024]{0:T(1024)S(1)} %convert_element_type.162, bf16[2048,2048]{1,0:T(8,128)(2,1)S(1)} %bitcast.70, ...), kind=kOutput, calls=%fused_computation.15 | convolution fusion | flops 8747219968 | bytes 41951232 | tf_op jit(solution)/shard_map/dot_general | solution.py:122
  333.8 10.1 %multiply_convert_fusion = bf16[2048,1024]{1,0:T(8,128)(2,1)} fusion(f32[2048,1024]{1,0:T(8,128)} %get-tuple-element.169, f32[2048,1024]{1,0:T(8,128)} %get-tuple-element.188, f32[1024]{0:T(1024)S(1)} %convert_element_type.162), kind=kLoop, calls=%fused_computation.17 | loop fusion | flops 8388608 | bytes 20975616 | tf_op jit(solution)/shard_map/convert_element_type | solution.py:176
  344.0 16.8 %fusion.12 = bf16[2048,1280]{0,1:T(8,128)(2,1)} fusion(bf16[2048,2048]{1,0:T(8,128)(2,1)} %all-gather.8.cloned.1.call-done, bf16[2048,1024]{1,0:T(8,128)(2,1)} %multiply_convert_fusion, bf16[512,256]{1,0:T(8,128)(2,1)S(1)} %copy-done.65, bf16[512,256]{1,0:T(8,128)(2,1)S(1)} %copy-done.63, bf16[512,256]{1,0:T(8,128)(2,1)S(1)} %copy-done.62, ...), kind=kOutput, calls=%fused_computation.34 | convolution fusion | flops 10766254080 | bytes 18874368 | tf_op jit(solution)/shard_map/gd,gf->df/dot_general | solution.py:280
  360.9 4.5 multiply_convert_fusion.1
  370.6 1.7 fusion.53
  373.8 2.1 fusion.23
  380.9 2.1 fusion.30
  383.1 8.2 convolution_convert_fusion.3
  391.4 9.3 %convolution_convert_fusion.2 = bf16[2048,1024]{0,1:T(8,128)(2,1)S(1)} fusion(bf16[2048,2048]{1,0:T(8,128)(2,1)S(1)} %bitcast.72, bf16[2048,1024]{1,0:T(8,128)(2,1)S(1)} %copy-done.64), kind=kOutput, calls=%fused_computation.45 | convolution fusion | flops 8592031744 | bytes 16777216 | tf_op jit(solution)/shard_map/gd,gf->df/dot_general | solution.py:267
  400.7 5.9 pad_maximum_fusion
  406.7 1.8 copy-done.26
  408.5 12.3 %fusion.25 = f32[2048,2048]{1,0:T(8,128)} fusion(bf16[2048,768]{0,1:T(8,128)(2,1)S(1)} %copy-done.26, bf16[2048,1792]{1,0:T(8,128)(2,1)} %all-gather.4.cloned.1.call-done), kind=kOutput, calls=%fused_computation.73 | convolution fusion | flops 6442450944 | bytes 23068672 | tf_op jit(solution)/shard_map/gf,df->gd/dot_general | solution.py:246
  420.7 26.8 %fusion.137 = (f32[2048]{0:T(1024)S(1)}, f32[2048]{0:T(1024)S(1)}, bf16[2048,2048]{1,0:T(8,128)(2,1)}, f32[2048]{0:T(1024)S(1)}, f32[2048]{0:T(1024)S(1)}) fusion(bf16[8,256,2048]{2,1,0:T(8,128)(2,1)} %gather_fusion, f32[2048]{0:T(1024)S(1)} %copy-done.48, f32[2048,2048]{1,0:T(8,128)} %fusion.25, f32[2048]{0:T(1024)S(1)} %copy-done.46, ...), kind=kOutput, calls=%fused_computation.253 | convolution fusion | flops 8636063744 | bytes 41992192 | tf_op jit(solution)/shard_map/gf,df->gd/dot_general | solution.py:249
  447.6 17.8 %convolution_convert_fusion = bf16[2048,2048]{1,0:T(8,128)(2,1)} fusion(bf16[1280,2048]{1,0:T(8,128)(2,1)} %all-gather.6.cloned.1.call-done, bf16[2048,1024]{1,0:T(8,128)(2,1)} %multiply_convert_fusion, bf16[512,256]{1,0:T(8,128)(2,1)} %fusion.56, bf16[512,256]{1,0:T(8,128)(2,1)} %fusion.55, bf16[512,256]{1,0:T(8,128)(2,1)} %convolution_convert_fusion.4, ...), kind=kOutput, calls=%fused_computation.31 | convolution fusion | flops 10767826944 | bytes 18874368 | tf_op jit(solution)/shard_map/dot_general | solution.py:178
  466.5 7.5 all-reduce.3
  478.0 3.3 reduce-scatter.9.cloned.1.call-done
  481.4 3.0 slice.436
  484.3 2.9 copy.42
  487.9 2.8 copy.41
  490.6 143.2 %reduce-scatter.7.cloned.1.call-done = bf16[256,2048]{1,0:T(8,128)(2,1)} async-done(((bf16[2048,2048]{1,0:T(8,128)(2,1)}), bf16[256,2048]{1,0:T(8,128)(2,1)}) %reduce-scatter.7.cloned.1.call-update) | async-done | bytes 1048592 | tf_op jit(solution)/shard_map/reduce_scatter | solution.py:257
  633.8 1.9 convert_reduce_fusion.2
  635.8 150.2 %reduce-scatter.5.cloned.1.call-done = bf16[256,2048]{1,0:T(8,128)(2,1)} async-done(((bf16[2048,2048]{1,0:T(8,128)(2,1)}), bf16[256,2048]{1,0:T(8,128)(2,1)}) %reduce-scatter.5.cloned.1.call-update) | async-done | bytes 1048592 | tf_op jit(solution)/shard_map/reduce_scatter | solution.py:183
  786.0 4.9 convert_reduce_fusion.4
  790.8 40.3 %all-reduce.2 = (f32[2048]{0:T(1024)}, f32[2048]{0:T(1024)}, f32[2048]{0:T(1024)}, f32[2048]{0:T(1024)}, f32[2048]{0:T(1024)S(1)}) all-reduce(f32[2048]{0:T(1024)S(1)} %get-tuple-element.171, f32[2048]{0:T(1024)S(1)} %get-tuple-element.172, f32[2048]{0:T(1024)S(1)} %get-tuple-element.155, ...), channel_id=1, replica_groups=mesh['dp'=4,'tensor'=8] {'dp','tensor'}, use_global_device_ids=true, to_apply=%region_21.22 | all-reduce | flops 10240 | bytes 81920 | tf_op jit(solution)/shard_map/psum | solution.py:300
  (256 shorter events, 47.9 us)
Async XLA Ops:
  7.2 217.0 %all-gather.4.cloned.1.call-start = ((), (), s32[]{:S(2)}) async-start(), calls=%async_computation.4 | async-start | bytes 9175040 | tf_op jit(solution)/shard_map/all_gather | solution.py:118
  10.2 79.0 %copy-start.42 = (s32[1,2048]{1,0:T(1,128)S(1)}, s32[1,2048]{1,0:T(1,128)}, u32[]{:S(2)}) copy-start(s32[1,2048]{1,0:T(1,128)} %param.36) | copy-start | bytes 24580
  10.2 136.7 %copy-start.61 = (bf16[1024]{0:T(1024)(128)(2,1)S(1)}, bf16[1024]{0:T(1024)(128)(2,1)}, u32[]{:S(2)}) copy-start(bf16[1024]{0:T(1024)(128)(2,1)} %param.46) | copy-start | bytes 6148
  10.3 136.7 %copy-start.54 = (bf16[2048]{0:T(1024)(128)(2,1)S(1)}, bf16[2048]{0:T(1024)(128)(2,1)}, u32[]{:S(2)}) copy-start(bf16[2048]{0:T(1024)(128)(2,1)} %param.37) | copy-start | bytes 12292
  10.3 136.7 %copy-start.55 = (bf16[2048]{0:T(1024)(128)(2,1)S(1)}, bf16[2048]{0:T(1024)(128)(2,1)}, u32[]{:S(2)}) copy-start(bf16[2048]{0:T(1024)(128)(2,1)} %param.39) | copy-start | bytes 12292
  10.3 137.1 %copy-start.56 = (bf16[2048]{0:T(1024)(128)(2,1)S(1)}, bf16[2048]{0:T(1024)(128)(2,1)}, u32[]{:S(2)}) copy-start(bf16[2048]{0:T(1024)(128)(2,1)} %param.38) | copy-start | bytes 12292
  10.3 137.1 %copy-start.57 = (bf16[2048]{0:T(1024)(128)(2,1)S(1)}, bf16[2048]{0:T(1024)(128)(2,1)}, u32[]{:S(2)}) copy-start(bf16[2048]{0:T(1024)(128)(2,1)} %param.40) | copy-start | bytes 12292
  10.3 137.2 %copy-start.60 = (bf16[1,768]{1,0:T(2,128)(2,1)S(1)}, bf16[1,768]{1,0:T(2,128)(2,1)}, u32[]{:S(2)}) copy-start(bf16[1,768]{1,0:T(2,128)(2,1)} %param.42) | copy-start | bytes 4612
  10.3 237.1 %all-gather.6.cloned.1.call-start = ((), (), s32[]{:S(2)}) async-start(), calls=%async_computation.5 | async-start | bytes 6553600 | tf_op jit(solution)/shard_map/all_gather | solution.py:180
  11.6 255.5 %all-gather.8.cloned.1.call-start = ((), (), s32[]{:S(2)}) async-start(), calls=%async_computation.7 | async-start | bytes 9437184 | tf_op jit(solution)/shard_map/all_gather | solution.py:189
  11.8 187.4 %copy-start.43 = (f32[256]{0:T(256)}, f32[256]{0:T(256)S(1)}, u32[]{:S(2)}) copy-start(f32[256]{0:T(256)S(1)} %broadcast_multiply_fusion.2) | copy-start | bytes 3076
  12.3 187.0 %copy-start.49 = (f32[256]{0:T(256)}, f32[256]{0:T(256)S(1)}, u32[]{:S(2)}) copy-start(f32[256]{0:T(256)S(1)} %add_rsqrt_fusion) | copy-start | bytes 3076
  12.6 29.2 %collective-permute-start = (bf16[256,2048]{1,0:T(8,128)(2,1)S(1)}, bf16[256,2048]{1,0:T(8,128)(2,1)S(1)}, u32[]{:S(2)}, u32[]{:S(2)}) collective-permute-start(bf16[256,2048]{1,0:T(8,128)(2,1)S(1)} %fusion.34), channel_id=1, source_target_pairs={{0,1},{1,2},{2,3},{3,4},{4,5},{5,6},{6,7},{7,0},{8,9},{9,10},{10,1... | collective-permute-start | bytes 3145736 | tf_op jit(solution)/shard_map/ppermute | solution.py:27
  41.8 44.6 %collective-permute-start.1 = (bf16[256,2048]{1,0:T(8,128)(2,1)S(1)}, bf16[256,2048]{1,0:T(8,128)(2,1)}, u32[]{:S(2)}, u32[]{:S(2)}) collective-permute-start(bf16[256,2048]{1,0:T(8,128)(2,1)S(1)} %collective-permute-done), channel_id=1, source_target_pairs={{0,1},{1,2},{2,3},{3,4},{4,5},{5,6},{6,7},{7,0},{8,9},{9,10},{10,1... | collective-permute-start | bytes 3145736 | tf_op jit(solution)/shard_map/ppermute | solution.py:27
  41.8 47.5 %collective-permute-start.4 = (bf16[256,2048]{1,0:T(8,128)(2,1)S(1)}, bf16[256,2048]{1,0:T(8,128)(2,1)}, u32[]{:S(2)}, u32[]{:S(2)}) collective-permute-start(bf16[256,2048]{1,0:T(8,128)(2,1)S(1)} %fusion.34), channel_id=1, source_target_pairs={{1,0},{2,1},{3,2},{4,3},{5,4},{6,5},{7,6},{0,7},{9,8},{10,9},{11,1... | collective-permute-start | bytes 3145736 | tf_op jit(solution)/shard_map/ppermute | solution.py:29
  86.4 58.0 %collective-permute-start.2 = (bf16[256,2048]{1,0:T(8,128)(2,1)}, bf16[256,2048]{1,0:T(8,128)(2,1)}, u32[]{:S(2)}, u32[]{:S(2)}) collective-permute-start(bf16[256,2048]{1,0:T(8,128)(2,1)} %collective-permute-done.1), channel_id=1, source_target_pairs={{0,1},{1,2},{2,3},{3,4},{4,5},{5,6},{6,7},{7,0},{8,9},{9,10},{10,1... | collective-permute-start | bytes 3145736 | tf_op jit(solution)/shard_map/ppermute | solution.py:27
  89.1 385.0 %reduce-scatter.11.cloned.1.call-start = ((), (), s32[]{:S(2)}) async-start(), calls=%async_computation.10 | async-start | bytes 6553600 | tf_op jit(solution)/shard_map/reduce_scatter | solution.py:279
  89.4 62.2 %collective-permute-start.5 = (bf16[256,2048]{1,0:T(8,128)(2,1)}, bf16[256,2048]{1,0:T(8,128)(2,1)S(1)}, u32[]{:S(2)}, u32[]{:S(2)}) collective-permute-start(bf16[256,2048]{1,0:T(8,128)(2,1)} %collective-permute-done.4), channel_id=1, source_target_pairs={{1,0},{2,1},{3,2},{4,3},{5,4},{6,5},{7,6},{0,7},{9,8},{10,9},{11,1... | collective-permute-start | bytes 3145736 | tf_op jit(solution)/shard_map/ppermute | solution.py:29
  144.4 46.5 %collective-permute-start.3 = (bf16[256,2048]{1,0:T(8,128)(2,1)}, bf16[256,2048]{1,0:T(8,128)(2,1)}, u32[]{:S(2)}, u32[]{:S(2)}) collective-permute-start(bf16[256,2048]{1,0:T(8,128)(2,1)} %collective-permute-done.2), channel_id=1, source_target_pairs={{0,1},{1,2},{2,3},{3,4},{4,5},{5,6},{6,7},{7,0},{8,9},{9,10},{10,1... | collective-permute-start | bytes 3145736 | tf_op jit(solution)/shard_map/ppermute | solution.py:27
  146.9 66.3 %copy-start.45 = (f32[2048]{0:T(1024)}, f32[2048]{0:T(1024)S(1)}, u32[]{:S(2)}) copy-start(f32[2048]{0:T(1024)S(1)} %convert_element_type.147) | copy-start | bytes 24580
  147.0 66.3 %copy-start.47 = (f32[2048]{0:T(1024)}, f32[2048]{0:T(1024)S(1)}, u32[]{:S(2)}) copy-start(f32[2048]{0:T(1024)S(1)} %convert_element_type.159) | copy-start | bytes 24580
  147.6 87.0 %copy-start.51 = (f32[32]{0:T(128)}, f32[32]{0:T(128)S(1)}, u32[]{:S(2)}) copy-start(f32[32]{0:T(128)S(1)} %multiply_power_fusion) | copy-start | bytes 388
  147.7 86.9 %copy-start.39 = (f32[2048]{0:T(1024)}, f32[2048]{0:T(1024)S(1)}, u32[]{:S(2)}) copy-start(f32[2048]{0:T(1024)S(1)} %fusion.134) | copy-start | bytes 24580
  151.6 52.4 %collective-permute-start.6 = (bf16[256,2048]{1,0:T(8,128)(2,1)S(1)}, bf16[256,2048]{1,0:T(8,128)(2,1)S(1)}, u32[]{:S(2)}, u32[]{:S(2)}) collective-permute-start(bf16[256,2048]{1,0:T(8,128)(2,1)S(1)} %collective-permute-done.5), channel_id=1, source_target_pairs={{1,0},{2,1},{3,2},{4,3},{5,4},{6,5},{7,6},{0,7},{9,8},{10,9},{11,1... | collective-permute-start | bytes 3145736 | tf_op jit(solution)/shard_map/ppermute | solution.py:29
  234.6 11.1 %copy-start.17 = (bf16[2048,768]{0,1:T(8,128)(2,1)}, bf16[2048,768]{0,1:T(8,128)(2,1)S(1)}, u32[]{:S(2)}) copy-start(bf16[2048,768]{0,1:T(8,128)(2,1)S(1)} %get-tuple-element.189) | copy-start | bytes 9437188
  267.0 17.1 %copy-start.11 = (f32[512,512]{0,1:T(8,128)S(1)}, f32[512,512]{0,1:T(8,128)}, u32[]{:S(2)}) copy-start(f32[512,512]{0,1:T(8,128)} %copy-done.10) | copy-start | bytes 3145732
  267.0 17.4 %copy-start.18 = (bf16[2048,768]{0,1:T(8,128)(2,1)S(1)}, bf16[2048,768]{0,1:T(8,128)(2,1)}, u32[]{:S(2)}) copy-start(bf16[2048,768]{0,1:T(8,128)(2,1)} %copy-done.17) | copy-start | bytes 9437188
  284.1 12.4 %copy-start.36 = (bf16[2048,1280]{1,0:T(8,128)(2,1)}, bf16[2048,1280]{1,0:T(8,128)(2,1)S(1)}, u32[]{:S(2)}) copy-start(bf16[2048,1280]{1,0:T(8,128)(2,1)S(1)} %get-tuple-element.191) | copy-start | bytes 15728644
  284.9 6.1 copy-start.6
  285.2 6.4 copy-start.19
  294.3 5.9 slice-start
  333.8 10.1 %copy-start.62 = (bf16[512,256]{1,0:T(8,128)(2,1)S(1)}, bf16[512,256]{1,0:T(8,128)(2,1)}, u32[]{:S(2)}) copy-start(bf16[512,256]{1,0:T(8,128)(2,1)} %convolution_convert_fusion.4) | copy-start | bytes 786436
  333.8 10.1 %copy-start.63 = (bf16[512,256]{1,0:T(8,128)(2,1)S(1)}, bf16[512,256]{1,0:T(8,128)(2,1)}, u32[]{:S(2)}) copy-start(bf16[512,256]{1,0:T(8,128)(2,1)} %fusion.55) | copy-start | bytes 786436
  333.8 10.1 %copy-start.65 = (bf16[512,256]{1,0:T(8,128)(2,1)S(1)}, bf16[512,256]{1,0:T(8,128)(2,1)}, u32[]{:S(2)}) copy-start(bf16[512,256]{1,0:T(8,128)(2,1)} %fusion.56) | copy-start | bytes 786436
  360.8 120.6 %reduce-scatter.9.cloned.1.call-start = ((), (), s32[]{:S(2)}) async-start(), calls=%async_computation.9 | async-start | bytes 9175040 | tf_op jit(solution)/shard_map/reduce_scatter | solution.py:263
  373.8 9.3 %slice-start.4 = ((s8[8388608]{0:T(1024)(128)(4,1)}), s8[4194304]{0:T(1024)(128)(4,1)S(1)}, s32[]{:S(2)}) async-start(s8[8388608]{0:T(1024)(128)(4,1)} %bitcast.73), calls=%async_computation.15 | async-start | bytes 8388608
  380.9 10.4 %slice-start.2 = ((s8[8388608]{0:T(1024)(128)(4,1)}), s8[4194304]{0:T(1024)(128)(4,1)S(1)}, s32[]{:S(2)}) async-start(s8[8388608]{0:T(1024)(128)(4,1)} %bitcast.71), calls=%async_computation.13 | async-start | bytes 8388608
  383.1 8.2 copy-start.25
  383.1 8.2 slice-start.3
  383.1 8.2 copy-start.64
  406.6 14.1 %copy-start.46 = (f32[2048]{0:T(1024)S(1)}, f32[2048]{0:T(1024)}, u32[]{:S(2)}) copy-start(f32[2048]{0:T(1024)} %copy-done.45) | copy-start | bytes 24580
  406.6 14.1 %copy-start.48 = (f32[2048]{0:T(1024)S(1)}, f32[2048]{0:T(1024)}, u32[]{:S(2)}) copy-start(f32[2048]{0:T(1024)} %copy-done.47) | copy-start | bytes 24580
  406.6 227.2 %reduce-scatter.7.cloned.1.call-start = ((), (), s32[]{:S(2)}) async-start(), calls=%async_computation.8 | async-start | bytes 9437184 | tf_op jit(solution)/shard_map/reduce_scatter | solution.py:257
  447.5 338.4 %reduce-scatter.5.cloned.1.call-start = ((), (), s32[]{:S(2)}) async-start(), calls=%async_computation.6 | async-start | bytes 9437184 | tf_op jit(solution)/shard_map/reduce_scatter | solution.py:183
  481.4 5.9 copy-start.12
  487.7 146.1 %copy-start.4 = (bf16[256,2048]{1,0:T(8,128)(2,1)S(1)}, bf16[256,2048]{1,0:T(8,128)(2,1)}, u32[]{:S(2)}) copy-start(bf16[256,2048]{1,0:T(8,128)(2,1)} %param.35) | copy-start | bytes 3145732
  487.7 146.1 %copy-start.44 = (f32[256]{0:T(256)S(1)}, f32[256]{0:T(256)}, u32[]{:S(2)}) copy-start(f32[256]{0:T(256)} %copy-done.43) | copy-start | bytes 3076
  487.7 146.1 %copy-start.50 = (f32[256]{0:T(256)S(1)}, f32[256]{0:T(256)}, u32[]{:S(2)}) copy-start(f32[256]{0:T(256)} %copy-done.49) | copy-start | bytes 3076
  (39 other events, 123.3 us)
Sparse Core Ops, SparseCore 0:
  10.3 55.0 all-gather.3
  67.6 40.4 all-gather.5
  110.2 156.8 all-gather.7
  360.9 52.1 reduce-scatter.10
  415.6 65.7 reduce-scatter.8
  484.8 148.9 reduce-scatter.6
  637.9 148.0 reduce-scatter.4
